TPU v7x, 128 devices: a whole 4x4x4 slice. The times are simulated.
128 devices in a mesh: span: 8 (over z, core), xs: 16 (over y, x).
Axes of the slice: x: 4, y: 4, z: 4, core: 2. Of those that a mesh axis runs over, the one named last changes fastest.
Arguments:
- source: float32 [64, 64, 4096], P(None, 'span', 'xs'), may hold values from -0.75 to 0.75
- coefficient: float32 [64, 64, 4096], P(None, 'span', 'xs'), may hold values from 2.5 to 5
- volume_matrix: float32 [64, 64], replicated, may hold values from -0.75 to 0.75
- span_lower: float32 [64, 64], replicated, may hold values from -0.375 to 0.375
- span_upper: float32 [64, 64], replicated, may hold values from -0.375 to 0.375
- cross_lower: float32 [64, 64], replicated, may hold values from -0.375 to 0.375
- cross_upper: float32 [64, 64], replicated, may hold values from -0.375 to 0.375
- interface: int32 [8, 16, 128], P('span', 'xs'), may hold values from 0 to 131071
- compliance: float32 [8, 2048, 2048], P('span', 'xs'), may hold values from -0.5 to 0.5
- start_displacement: float32 [8, 16, 128], P('span', 'xs'), may hold values from -8 to 8
Outputs:
- fluid_state: float32 [64, 64, 4096], P(None, 'span', 'xs')
- shell_displacement: float32 [8, 16, 128], P('span', 'xs')
All inputs are finite; a program needn't handle non-finite values.
Results may differ from a plain program's by a relative error of at most 0.0001.
Values sent between devices are 32-bit elements; how exact they have to be, the bound alone decides.
No kernel may reach another device: no remote copies, remote signals or barrier semaphores. Data moves between devices by JAX's collectives and lax.ppermute only.
A program may use at most 64 MiB of HBM per device.

v0:
```python
import jax
import jax.numpy as jnp
from jax import lax
from jax.experimental import pallas as pl
from jax.experimental.pallas import tpu as pltpu
from jax.sharding import PartitionSpec as P


NODES, ES, EX, IFN = 64, 8, 256, 128
LANES = EX + 128
AXES = ("span", "xs")
THETA = 3.75
f32 = jnp.float32
bf16 = jnp.bfloat16
NT = (((1,), (1,)), ((), ()))


def parts(x):
    hi = x.astype(bf16)
    return hi, (x - hi.astype(f32)).astype(bf16)


def place(i):
    i = i.astype(jnp.int32)
    return i >> 11, (i >> 8) & 7, i & 255


def onehot(pos, size):
    rows = lax.broadcasted_iota(jnp.int32, (size, IFN), 0)
    return rows == pos


def pick(mask):
    return jnp.where(mask, 1.0, 0.0).astype(bf16)


def lane_rows(entries):
    rows = lax.broadcasted_iota(jnp.int32, (128, 128), 0)
    tile = jnp.zeros((128, 128), f32)
    for pos, value in entries:
        tile = jnp.where(rows == pos, value, tile)
    return tile.T


def at(s, first=0):
    return slice((s - first) * NODES, (s - first + 1) * NODES)


def position():
    return lax.axis_index("span"), lax.axis_index("xs")


def pack(*refs):
    far, (columns, edge_a, edge_b, *near, halves, sems) = refs[:9], refs[9:]
    src, cf, own, disp, *_ = near
    pairs = [(f.at[:, pl.ds(h * 128, 128)], halves.at[2 * k + h]) for k, f in enumerate(far[:2]) for h in (0, 1)]
    pairs += list(zip(far[2:], near[2:]))
    copies = [pltpu.make_async_copy(a, b, sems.at[k]) for k, (a, b) in enumerate(pairs)]
    for copy in copies:
        copy.start()
    lane = lax.broadcasted_iota(jnp.int32, (1, 128), 1)
    tile = jnp.zeros((2 * NODES, 128), f32)
    for k, (ref, wide, base) in enumerate(((src, 2, 0), (cf, 1, 16))):
        copies[2 * k].wait()
        copies[2 * k + 1].wait()
        for p in range(4):
            slot = base + 2 * wide * p
            low, high = (
                jnp.concatenate([halves[2 * k + h, pl.ds(2 * p + e, NODES, stride=ES), :] for e in (0, 1)], 0)
                for h in (0, 1)
            )
            rows = slice(2 * p * NODES, (2 * p + 2) * NODES)
            ref[rows, :128] = low
            ref[rows, 128:] = high
            ends = pltpu.roll(jnp.where(lane < NODES, low, high), slot + wide, 1)
            tile = jnp.where((lane >= slot) & (lane < slot + 2 * wide), ends, tile)
    for copy in copies[4:]:
        copy.wait()
    columns[...] = tile.T[:32]
    columns[24:25] = own[...].astype(f32)
    columns[25:26] = disp[...]
    span, _ = position()
    for out, top in ((edge_a, span % 2 == 0), (edge_b, span % 2 == 1)):

        @pl.when(top)
        def _():
            out[: 2 * NODES] = src[(ES - 2) * NODES :, :]
            out[2 * NODES :] = cf[(ES - 1) * NODES :, :]

        @pl.when(jnp.logical_not(top))
        def _():
            out[: 2 * NODES] = src[: 2 * NODES, :]
            out[2 * NODES :] = cf[:NODES, :]


def sides(index, first, second):
    even = index % 2 == 0
    return jnp.where(even, second, first), jnp.where(even, first, second)


def pack_corner(cross_a, cross_b, own, disp, first, second):
    span, cross = position()
    half = lax.broadcasted_iota(jnp.int32, (1, 128), 1) < NODES
    left, right = sides(cross, cross_a[...], cross_b[...])
    after = jnp.where(half, pltpu.roll(left[13:14], NODES, 1), right[14:15])
    before = jnp.where(half, left[1:2], pltpu.roll(right[2:3], NODES, 1))
    rows = [left[24:25], own[...].astype(f32), right[24:25], left[25:26], disp[...], right[25:26]]
    rows = jnp.concatenate(rows + [jnp.zeros((1, 128), f32)], 0)
    for out, top in ((first, span % 2 == 0), (second, span % 2 == 1)):
        out[0:1] = jnp.where(top, after, before)
        out[1:8] = rows


def join(cross_a, cross_b, d, out):
    dl, dr = sides(position()[1], cross_a[...], cross_b[...])
    out[...] = jnp.concatenate([dl, d[...], dr], 0)


def product(mats, x, lo, hi):
    xh, xl = parts(x)
    return jnp.dot(
        mats[lo * NODES : hi * NODES, :], jnp.concatenate([xh, xh, xl], 0), preferred_element_type=f32
    )


def spread(sel, cols):
    return lax.dot_general(
        jnp.concatenate(sel, 1), jnp.concatenate(cols, 1), NT, preferred_element_type=f32
    )


def weighted(x, size, value):
    return parts(jnp.where(onehot(x, size), value, 0.0))


def main_part(spot, shift, size, d):
    n, s, x = spot
    sel = pick(onehot((s + shift) * NODES + n, size))
    return spread([sel, sel], weighted(x, EX, d))


def side_part(before, after, shift, size, d_before, d_after):
    (nb, sb, xb), (na, sa, xa) = before, after
    sel_b = pick(onehot((sb + shift) * NODES + nb, size))
    sel_a = pick(onehot((sa + shift) * NODES + na, size))
    cols_b = weighted(jnp.where(xb >= EX - 2, xb - 128, -1), 128, d_before)
    cols_a = weighted(jnp.where(xa < 2, xa, -1), 128, d_after)
    return spread([sel_b, sel_b, sel_a, sel_a], cols_b + cols_a)


def trace(field, spot):
    n, s, x = spot
    cols = pick(onehot(x, EX))
    found = jnp.dot(
        jnp.concatenate(parts(field), 1), jnp.concatenate([cols, cols], 0), preferred_element_type=f32
    )
    return jnp.sum(jnp.where(onehot(s * NODES + n, ES * NODES), found, 0.0), axis=0, keepdims=True)


def inner_kernel(first, *refs):
    if first:
        src, cf, own, disp, *raw, r_out, v_out, tr_out, mats = refs
        for k, ref in enumerate(raw):
            m = ref[...] if k == 0 else -ref[...]
            high = m.astype(bf16).astype(f32)
            mats[at(k), :] = jnp.concatenate([high, m - high, high], 1).astype(bf16)
    else:
        src, cf, own, disp, mats, r_out, v_out, tr_out = refs
    spot = place(own[...])
    r_out[...] = src[...] + main_part(spot, 0, ES * NODES, disp[...])
    lane = lax.broadcasted_iota(jnp.int32, (1, EX), 1)
    low, pending = None, None
    for s in range(ES):
        prod = product(mats, r_out[at(s), :], 0, 5)
        up = prod[2 * NODES : 3 * NODES]
        if s:
            v_out[at(s), :EX] = pending + up
        else:
            v_out[at(0), :EX] = up
        before = pltpu.roll(prod[3 * NODES : 4 * NODES], 1, 1)
        after = pltpu.roll(prod[4 * NODES :], EX - 1, 1)
        pending = (
            cf[at(s), :] * r_out[at(s), :] + prod[:NODES]
            + jnp.where(lane == 0, 0.0, before) + jnp.where(lane == EX - 1, 0.0, after)
        )
        if s:
            pending = pending + low
        v_out[at(s + 1), EX:] = jnp.where(lane[:, :128] == 0, before[:, :128], 0.0) + jnp.where(
            lane[:, :128] == 127, after[:, 128:], 0.0
        )
        low = prod[NODES : 2 * NODES]
    v_out[at(ES), :EX] = pending
    v_out[at(ES + 1), :EX] = low
    tr_out[...] = trace(r_out[...], spot)


def lines(prod, k):
    return prod[k * NODES : (k + 1) * NODES]


def cast(before, after):
    lane = lax.broadcasted_iota(jnp.int32, (1, 128), 1)
    first_lane = jnp.where(lane == 0, pltpu.roll(before, 1, 1), 0.0)
    last_lane = jnp.where(lane == 127, pltpu.roll(after, 127, 1), 0.0)
    return jnp.concatenate([first_lane, last_lane], 1)


def kept_lanes(cross, n_xs):
    lane = lax.broadcasted_iota(jnp.int32, (1, 128), 1)
    return jnp.where((lane == 0) & (cross < n_xs - 1) | (lane == 127) & (cross > 0), 1.0, 0.0).astype(f32)


def side_kernel(first, n_xs, *refs):
    _, cross = position()
    part, mats, cross_a, cross_b, *refs = refs
    left, right = sides(cross, cross_a[...], cross_b[...])
    if first:
        out, wing, edge, w_scr = refs
        d_left, d_right = left[25:26], right[25:26]
        for p in range(4):
            k, rows = 4 * p, slice(2 * p * NODES, (2 * p + 2) * NODES)
            wing[rows, :] = lane_rows(
                ((0, right[k + 2 : k + 3]), (1, right[k + 3 : k + 4]), (126, left[k : k + 1]), (127, left[k + 1 : k + 2]))
            )
            k = 16 + 2 * p
            edge[rows, :] = lane_rows(((0, right[k + 1 : k + 2]), (127, left[k : k + 1])))
    else:
        d_ca, d_cb, wing, edge, out, w_scr = refs
        d_left, d_right = sides(cross, d_ca[...], d_cb[...])
    w_scr[...] = wing[...] + side_part(
        place(left[24:25]), place(right[24:25]), 0, ES * NODES, d_left, d_right
    )
    lane = lax.broadcasted_iota(jnp.int32, (1, 128), 1)
    keep = kept_lanes(cross, n_xs)
    out[at(0), :EX] = part[at(0), :EX]
    out[at(9), :EX] = part[at(9), :EX]

    def pair(s):
        both = product(mats, jnp.concatenate([w_scr[at(s), :], w_scr[at(s + 1), :]], 1), 0, 5)
        return both[:, :128], both[:, 128:]

    old, now = None, pair(0)
    for s in range(0, ES, 2):
        new = pair(s + 2) if s + 2 < ES else None
        for k, prod, down, up in (
            (s, now[0], old and old[1], now[1]), (s + 1, now[1], now[0], new and new[0]),
        ):
            out[at(k + 1), :EX] = part[at(k + 1), :EX] + cast(lines(prod, 3), lines(prod, 4))
            outer = (
                edge[at(k), :] * w_scr[at(k), :] + lines(prod, 0)
                + jnp.where(lane == 0, 0.0, pltpu.roll(lines(prod, 3), 1, 1))
                + jnp.where(lane == 127, 0.0, pltpu.roll(lines(prod, 4), 127, 1))
            )
            if down is not None:
                outer = outer + lines(down, 1)
            if up is not None:
                outer = outer + lines(up, 2)
            out[at(k + 1), EX:] = (part[at(k + 1), EX:] + outer) * keep
        old, now = now, new


def outer_kernel(first, n_xs, *refs):
    span, cross = position()
    cf, r_own, part, tr, mats, small_a, small_b, own, *refs = refs
    i_bel, i_abv = sides(span, small_a[...], small_b[...])
    if first:
        edge_a, edge_b, msg, rim, wing, h_scr, v_scr = refs
        d_bel, d_abv = i_bel[4:7], i_abv[4:7]
        rim[: 3 * NODES], rim[3 * NODES :] = sides(span, edge_a[...], edge_b[...])
        half = lax.broadcasted_iota(jnp.int32, (1, 128), 1) < NODES
        cb, ct = i_bel[0:1], i_abv[0:1]
        wing[...] = lane_rows(
            (
                (0, jnp.where(half, pltpu.roll(cb, NODES, 1), ct)),
                (127, jnp.where(half, cb, pltpu.roll(ct, NODES, 1))),
            )
        )
    else:
        d_a, d_b, rim, wing, msg, v_out, h_scr, v_scr = refs
        d_bel, d_abv = sides(span, d_a[...], d_b[...])
    spot = place(own[...])
    corners = []
    for idx, d, shift, base, turn in ((i_bel, d_bel, 2 - ES, 0, 1 - ES), (i_abv, d_abv, 0, 3 * NODES, 0)):
        spots = [place(idx[k : k + 1]) for k in (1, 2, 3)]
        h_scr[slice(base, base + 2 * NODES), :] = rim[base : base + 2 * NODES] + main_part(
            spots[1], shift, 2 * NODES, d[1:2]
        )
        corners.append(side_part(spots[0], spots[2], turn, NODES, d[0:1], d[2:3]))
    far_b = product(mats, h_scr[at(0), :], 1, 2)
    near_b = product(mats, h_scr[at(1), :], 0, 5)
    near_a = product(mats, h_scr[at(3), :], 0, 5)
    far_a = product(mats, h_scr[at(4), :], 2, 3)
    ends = product(
        mats, jnp.concatenate([wing[at(0), :] + corners[0], wing[at(1), :] + corners[1]], 1), 1, 5
    )
    lane = lax.broadcasted_iota(jnp.int32, (1, 128), 1)
    wide = lax.broadcasted_iota(jnp.int32, (1, EX), 1)
    keep = kept_lanes(cross, n_xs)

    def shifted(prod):
        return jnp.where(wide == 0, 0.0, pltpu.roll(lines(prod, 3), 1, 1)) + jnp.where(
            wide == EX - 1, 0.0, pltpu.roll(lines(prod, 4), EX - 1, 1)
        )

    for s, k, prod, far, lanes in (
        (1, 1, near_b, far_b, slice(0, 128)), (10, 3, near_a, far_a, slice(128, 256)),
    ):
        coef = rim[2 * NODES : 3 * NODES] if s == 1 else rim[5 * NODES :]
        v_scr[at(s, 1), :EX] = (
            part[at(s, 1), :EX] + coef * h_scr[at(k), :] + lines(prod, 0) + far + shifted(prod)
            + cast(ends[2 * NODES : 3 * NODES, lanes], ends[3 * NODES :, lanes])
        )
    v_scr[at(2, 1), :EX] = part[at(2, 1), :EX] + lines(near_b, 1)
    v_scr[at(2, 1), EX:] = part[at(2, 1), EX:] + lines(ends, 0)[:, :128] * keep
    v_scr[at(9, 1), :EX] = part[at(9, 1), :EX] + lines(near_a, 2)
    v_scr[at(9, 1), EX:] = part[at(9, 1), EX:] + lines(ends, 1)[:, 128:] * keep
    v_scr[at(3, 1).start : at(8, 1).stop, :] = part[at(3, 1).start : at(8, 1).stop, :]

    casts = {}
    for s in range(2, 10, 2):
        pair = product(mats, jnp.concatenate([v_scr[at(s, 1), EX:], v_scr[at(s + 1, 1), EX:]], 1), 3, 5)
        casts[s] = cast(pair[:NODES, :128], pair[NODES:, :128])
        casts[s + 1] = cast(pair[:NODES, 128:], pair[NODES:, 128:])
    sums = [jnp.zeros((8, EX), f32) for _ in range(5)]
    low = product(mats, v_scr[at(1, 1), :EX], 1, 2)
    pending = None
    for s in range(2, 11):
        if s < 10:
            prod = product(mats, v_scr[at(s, 1), :EX], 0, 5)
            up = lines(prod, 2)
        else:
            up = product(mats, v_scr[at(s, 1), :EX], 2, 3)
        if pending is not None:
            r, v = r_own[at(s - 1, 2), :], v_scr[at(s - 1, 1), :EX]
            w = pending + up - THETA * v
            pairs = ((v, v), (v, w), (w, w), (r, v), (r, w))
            for k, (a, b) in enumerate(pairs):
                sums[k] = sums[k] + jnp.sum((a * b).reshape(8, 8, EX), axis=0)
        if s < 10:
            pending = (
                cf[at(s, 2), :] * v_scr[at(s, 1), :EX] + lines(prod, 0) + low + casts[s] + shifted(prod)
            )
            low = lines(prod, 1)

    gram = jnp.zeros((1, 128), f32)
    for k in range(5):
        total = jnp.sum(jnp.sum(sums[k], axis=0, keepdims=True), axis=1, keepdims=True)
        gram = gram + jnp.where(lane == k, total, 0.0)
    v_mid = v_scr[NODES : 9 * NODES, :EX]
    rows = [gram, tr[...], trace(v_mid, spot)]
    msg[...] = jnp.broadcast_to(jnp.concatenate(rows, 1)[None], msg.shape)
    if not first:
        v_out[...] = v_mid


def solve(got):
    total = jnp.sum(got[:, 0, :128], axis=0, keepdims=True)
    lane = lax.broadcasted_iota(jnp.int32, (1, 128), 1)
    g11, g12, g22, g1, g2 = (
        jnp.sum(jnp.where(lane == k, total, 0.0), axis=1, keepdims=True) for k in range(5)
    )
    ratio = g12 / g11
    b = (g2 - ratio * g1) / (g22 - ratio * g12)
    a = (g1 - b * g12) / g11
    return a - THETA * b, b


def displace(a, b, got, compliance, disp, out):
    start = position()[0] * 16
    traces = a * got[pl.ds(start, 16), 0, 128:256] + b * got[pl.ds(start, 16), 0, 256:]
    acc = jnp.zeros((IFN, 128), f32)
    for j in range(16):
        acc = acc + compliance[:, j * 128 : (j + 1) * 128] * traces[j : j + 1]
    fresh = jnp.sum(acc.T, axis=0, keepdims=True)
    out[...] = 0.5 * fresh + 0.5 * disp[...]


def shell_kernel(got, compliance, disp, out):
    displace(*solve(got), got, compliance, disp, out)


def final_kernel(got, compliance, disp, r, v, fluid, out):
    a, b = solve(got)
    displace(a, b, got, compliance, disp, out)
    for s in range(ES):
        fluid[:, s, :] = a * r[at(s), :] + b * v[at(s), :]


def call(kernel, outs, ins, scratch=()):
    vm = pl.BlockSpec(memory_space=pltpu.VMEM)
    return pl.pallas_call(
        kernel,
        out_shape=[pltpu.VMEM(*o) for o in outs],
        in_specs=[vm] * len(ins),
        out_specs=[vm] * len(outs),
        scratch_shapes=[pltpu.VMEM(x, f32) for x in scratch],
        compiler_params=pltpu.CompilerParams(vmem_limit_bytes=16 << 20),
    )(*(pltpu.with_memory_space_constraint(x, pltpu.VMEM) for x in ins))


def swaps(axis, wrap):
    size = lax.axis_size(axis)
    pairs = [(i, i + 1) for i in range(size - 1)] + ([(size - 1, 0)] if wrap else [])
    return [[p for i, j in pairs[k::2] for p in ((i, j), (j, i))] for k in (0, 1)]


def body(
    source, coefficient, volume_matrix, span_lower, span_upper, cross_lower,
    cross_upper, interface, compliance, start_displacement,
):
    n_xs = lax.axis_size("xs")
    own, disp, rows = interface[0], start_displacement[0], compliance[0]
    mats = [volume_matrix, span_lower, span_upper, cross_lower, cross_upper]
    message, block = ((128, 1, 3 * 128), f32), ((ES * NODES, EX), f32)
    row, wide = ((1, 128), f32), ((10 * NODES, LANES), f32)

    def trade(axis, a, b):
        first, second = swaps(axis, axis == "span")
        far = lax.ppermute(b, axis, second)
        near = lax.ppermute(a, axis, first)
        return [near, far]

    args = [x.reshape(ES * NODES, EX) for x in (source, coefficient)] + [own, disp] + mats
    far = pl.BlockSpec(memory_space=pl.ANY)
    packed, near_s, far_s, src, cf, own, disp, *mats = pl.pallas_call(
        pack,
        out_shape=[pltpu.VMEM((32, 128), f32)]
        + [pltpu.VMEM((3 * NODES, EX), f32)] * 2
        + [pltpu.VMEM(*block)] * 2
        + [pltpu.VMEM(x.shape, x.dtype) for x in args[2:]],
        in_specs=[far] * 9,
        out_specs=[pl.BlockSpec(memory_space=pltpu.VMEM)] * 12,
        scratch_shapes=[
            pltpu.VMEM((4, ES * NODES, 128), f32), pltpu.SemaphoreType.DMA((11,))
        ],
        compiler_params=pltpu.CompilerParams(vmem_limit_bytes=16 << 20),
        name="pack",
    )(*(pltpu.with_memory_space_constraint(x, pltpu.HBM) for x in args))
    ends = trade("span", near_s, far_s)
    cols = trade("xs", packed, packed)
    r, part, tr, split = call(
        lambda *refs: inner_kernel(True, *refs),
        [block, wide, row, ((5 * NODES, 3 * NODES), bf16)],
        [src, cf, own, disp, *mats],
    )
    small = call(pack_corner, [((8, 128), f32)] * 2, [*cols, own, disp])
    around = [*trade("span", *small), own]
    outers = ((ES * NODES, 128), f32)
    scratch = [(5 * NODES, EX), wide[0]]
    part, *cross = call(
        lambda *refs: side_kernel(True, n_xs, *refs), [wide, outers, outers],
        [part, split, *cols], [outers[0]],
    )
    sent, *static = call(
        lambda *refs: outer_kernel(True, n_xs, *refs),
        [message, ((6 * NODES, EX), f32), ((2 * NODES, 128), f32)],
        [cf, r, part, tr, split, *around, *ends], scratch,
    )
    got = lax.all_to_all(sent, AXES, 0, 0, tiled=True)
    (disp,) = call(shell_kernel, [row], [got, rows, disp])
    beside = trade("xs", disp, disp)
    r, part, tr = call(
        lambda *refs: inner_kernel(False, *refs),
        [block, wide, row], [src, cf, own, disp, split],
    )
    (mid,) = call(join, [((3, 128), f32)], [*beside, disp])
    over = trade("span", mid, mid)
    (part,) = call(
        lambda *refs: side_kernel(False, n_xs, *refs), [wide],
        [part, split, *cols, *beside, *cross], [outers[0]],
    )
    sent, v = call(
        lambda *refs: outer_kernel(False, n_xs, *refs), [message, block],
        [cf, r, part, tr, split, *around, *over, *static], scratch,
    )
    got = lax.all_to_all(sent, AXES, 0, 0, tiled=True)
    near = pl.BlockSpec(memory_space=pltpu.VMEM)
    fluid, disp = pl.pallas_call(
        final_kernel,
        out_shape=[jax.ShapeDtypeStruct((NODES, ES, EX), f32), jax.ShapeDtypeStruct(*row)],
        in_specs=[near] * 5,
        out_specs=[near] * 2,
        compiler_params=pltpu.CompilerParams(vmem_limit_bytes=16 << 20),
        name="final",
    )(*(pltpu.with_memory_space_constraint(x, pltpu.VMEM) for x in (got, rows, disp, r, v)))
    return fluid, disp[None]


def solution(mesh):
    field = P(None, "span", "xs")
    section = P("span", "xs", None)
    return jax.shard_map(
        body,
        mesh=mesh,
        in_specs=(field, field, P(), P(), P(), P(), P(), section, section, section),
        out_specs=(field, section),
        check_vma=False,
    )
```

profile of v0, /device:TPU:1, one launch (start us, length us, event | category | flops | bytes accessed | tf_op | source)
XLA Modules:
  0.0 68.7 jit_solution(9797905193091535000)
XLA Ops:
  0.6 1.6 %pack.1 = (f32[32,128]{1,0:T(8,128)S(1)}, f32[192,256]{1,0:T(8,128)S(1)}, f32[192,256]{1,0:T(8,128)S(1)}, f32[512,256]{1,0:T(8,128)S(1)}, f32[512,256]{1,0:T(8,1...) custom-call(f32[512,256]{1,0:T(8,128)} %bitcast.8, ...), custom_call_target="tpu_custom_call" | custom-call | tf_op jit(solution)/shard_map/pack/pallas_call | solution.py:425
  2.2 1.4 %collective-permute-start.4 = (f32[192,256]{1,0:T(8,128)S(1)}, f32[192,256]{1,0:T(8,128)S(1)}, u32[]{:S(2)}, u32[]{:S(2)}) collective-permute-start(f32[192,256]{1,0:T(8,128)S(1)} %get-tuple-element.50), channel_id=1, source_target_pairs={{0,16},{16,0},{32,48},{48,32},{64,80},{80,64},{96,112},{112,96},{1... | collective-permute-start | bytes 589832 | tf_op jit(solution)/shard_map/ppermute | solution.py:420
  3.7 1.7 %collective-permute-start.5 = (f32[192,256]{1,0:T(8,128)S(1)}, f32[192,256]{1,0:T(8,128)S(1)}, u32[]{:S(2)}, u32[]{:S(2)}) collective-permute-start(f32[192,256]{1,0:T(8,128)S(1)} %get-tuple-element.51), channel_id=1, source_target_pairs={{16,32},{32,16},{48,64},{64,48},{80,96},{96,80},{112,0},{0,112},{1... | collective-permute-start | bytes 589832 | tf_op jit(solution)/shard_map/ppermute | solution.py:419
  5.4 1.2 %collective-permute-start = (f32[32,128]{1,0:T(8,128)S(1)}, f32[32,128]{1,0:T(8,128)S(1)}, u32[]{:S(2)}, u32[]{:S(2)}) collective-permute-start(f32[32,128]{1,0:T(8,128)S(1)} %get-tuple-element.45), channel_id=1, source_target_pairs={{0,1},{1,0},{2,3},{3,2},{4,5},{5,4},{6,7},{7,6},{8,9},{9,8},{10,11... | collective-permute-start | bytes 49160 | tf_op jit(solution)/shard_map/ppermute | solution.py:420
  6.6 0.7 collective-permute-start.1
  7.3 0.7 %collective-permute-done.refs_2_.cross_a = f32[32,128]{1,0:T(8,128)S(1)} collective-permute-done((f32[32,128]{1,0:T(8,128)S(1)}, f32[32,128]{1,0:T(8,128)S(1)}, u32[]{:S(2)}, u32[]{:S(2)}) %collective-permute-start) | collective-permute-done | bytes 16416 | tf_op jit(solution)/shard_map/ppermute | solution.py:420
  8.0 0.0 collective-permute-done.1.refs_3_.cross_b
  8.0 0.1 shard_map.115
  8.1 3.7 %collective-permute-start.2 = (f32[8,128]{1,0:T(8,128)S(1)}, f32[8,128]{1,0:T(8,128)S(1)}, u32[]{:S(2)}, u32[]{:S(2)}) collective-permute-start(f32[8,128]{1,0:T(8,128)S(1)} %get-tuple-element.48), channel_id=1, source_target_pairs={{0,16},{16,0},{32,48},{48,32},{64,80},{80,64},{96,112},{112,96},{1... | collective-permute-start | bytes 12296 | tf_op jit(solution)/shard_map/ppermute | solution.py:420
  11.8 0.0 collective-permute-start.3
  11.8 1.1 %shard_map.113 = (f32[512,256]{1,0:T(8,128)S(1)}, f32[640,384]{1,0:T(8,128)S(1)}, f32[1,128]{1,0:T(1,128)S(1)}, bf16[320,192]{1,0:T(8,128)(2,1)S(1)}) custom-call(f32[512,256]{1,0:T(8,128)S(1)} %get-tuple-element.34.refs_0_, f32[512,256]{1,0:T(8,128)S(1)} %get-tuple-element.33.refs_1_.refs_0_, s32[1,128]{1,0:T(1,128)S(1)} %get-tuple-element.35.refs_2_.own.refs_7_, ...), custom_call_target="tpu_custom_call" | custom-call | tf_op jit(solution)/shard_map/pallas_call | solution.py:391
  12.9 0.7 shard_map.114
  13.5 0.0 collective-permute-done.2.refs_5_
  13.6 1.3 %collective-permute-done.3.refs_6_ = f32[8,128]{1,0:T(8,128)S(1)} collective-permute-done((f32[8,128]{1,0:T(8,128)S(1)}, f32[8,128]{1,0:T(8,128)S(1)}, u32[]{:S(2)}, u32[]{:S(2)}) %collective-permute-start.3) | collective-permute-done | bytes 4128 | tf_op jit(solution)/shard_map/ppermute | solution.py:419
  14.8 0.0 collective-permute-done.4.refs_8_
  14.8 0.0 collective-permute-done.5.refs_9_
  14.8 0.0 copy-start
  14.8 1.7 %shard_map.116 = (f32[128,1,384]{2,1,0:T(1,128)S(1)}, f32[384,256]{1,0:T(8,128)S(1)}, f32[128,128]{1,0:T(8,128)S(1)}) custom-call(f32[512,256]{1,0:T(8,128)S(1)} %get-tuple-element.33.refs_1_.refs_0_, f32[512,256]{1,0:T(8,128)S(1)} %get-tuple-element.42.refs_1_, f32[640,384]{1,0:T(8,128)S(1)} %get-tuple-element.46.refs_2_, ...), custom_call_target="tpu_custom_call" | custom-call | tf_op jit(solution)/shard_map/pallas_call | solution.py:391
  16.5 22.8 %all_to_all.10.got = f32[128,1,384]{2,1,0:T(1,128)S(1)} all-to-all(f32[128,1,384]{2,1,0:T(1,128)S(1)} %get-tuple-element.52), channel_id=1, replica_groups=mesh['span'=8,'xs'=16] {'span','xs'}, dimensions={0} | all-to-all | bytes 393216 | tf_op jit(solution)/shard_map/all_to_all | solution.py:459
  39.3 0.0 copy-done
  39.3 0.3 shard_map.117.refs_3_.d.disp
  39.6 0.4 collective-permute-start.6
  40.0 0.6 collective-permute-start.7
  40.7 1.5 %collective-permute-done.6.refs_4_.cross_a = f32[1,128]{1,0:T(1,128)S(1)} collective-permute-done((f32[1,128]{1,0:T(1,128)S(1)}, f32[1,128]{1,0:T(1,128)S(1)}, u32[]{:S(2)}, u32[]{:S(2)}) %collective-permute-start.6) | collective-permute-done | bytes 544 | tf_op jit(solution)/shard_map/ppermute | solution.py:420
  42.1 0.0 collective-permute-done.7.refs_5_.cross_b
  42.1 1.9 %collective-permute-start.8 = (f32[3,128]{1,0:T(4,128)S(1)}, f32[3,128]{1,0:T(4,128)S(1)}, u32[]{:S(2)}, u32[]{:S(2)}) collective-permute-start(f32[3,128]{1,0:T(4,128)S(1)} %shard_map.120), channel_id=1, source_target_pairs={{0,16},{16,0},{32,48},{48,32},{64,80},{80,64},{96,112},{112,96},{1... | collective-permute-start | bytes 4616 | tf_op jit(solution)/shard_map/ppermute | solution.py:420
  44.0 0.5 collective-permute-start.9
  44.6 1.1 %shard_map.118 = (f32[512,256]{1,0:T(8,128)S(1)}, f32[640,384]{1,0:T(8,128)S(1)}, f32[1,128]{1,0:T(1,128)S(1)}) custom-call(f32[512,256]{1,0:T(8,128)S(1)} %get-tuple-element.34.refs_0_, f32[512,256]{1,0:T(8,128)S(1)} %get-tuple-element.33.refs_1_.refs_0_, s32[1,128]{1,0:T(1,128)S(1)} %get-tuple-element.35.refs_2_.own.refs_7_, ...), custom_call_target="tpu_custom_call" | custom-call | tf_op jit(solution)/shard_map/pallas_call | solution.py:391
  45.7 0.7 shard_map.119.refs_2_
  46.3 0.0 collective-permute-done.8.refs_8_
  46.3 0.7 %collective-permute-done.9.refs_9_ = f32[3,128]{1,0:T(4,128)S(1)} collective-permute-done((f32[3,128]{1,0:T(4,128)S(1)}, f32[3,128]{1,0:T(4,128)S(1)}, u32[]{:S(2)}, u32[]{:S(2)}) %collective-permute-start.9) | collective-permute-done | bytes 1568 | tf_op jit(solution)/shard_map/ppermute | solution.py:419
  47.0 1.6 %shard_map.121 = (f32[128,1,384]{2,1,0:T(1,128)S(1)}, f32[512,256]{1,0:T(8,128)S(1)}) custom-call(f32[512,256]{1,0:T(8,128)S(1)} %get-tuple-element.33.refs_1_.refs_0_, f32[512,256]{1,0:T(8,128)S(1)} %get-tuple-element.53.refs_1_.r, f32[640,384]{1,0:T(8,128)S(1)} %shard_map.119.refs_2_, f32[1,128]{1,0:T(1,128)S(1)} %get-tuple-element.57.refs_3_, ...), custom_call_target="tpu_custom_call" | custom-call | tf_op jit(solution)/shard_map/pallas_call | solution.py:391
  48.7 18.8 %all_to_all.11.got = f32[128,1,384]{2,1,0:T(1,128)S(1)} all-to-all(f32[128,1,384]{2,1,0:T(1,128)S(1)} %get-tuple-element.60), channel_id=1, replica_groups=mesh['span'=8,'xs'=16] {'span','xs'}, dimensions={0} | all-to-all | bytes 393216 | tf_op jit(solution)/shard_map/all_to_all | solution.py:476
  67.5 1.3 %final.1 = (f32[64,8,256]{2,1,0:T(8,128)}, f32[1,128]{1,0:T(1,128)}) custom-call(f32[128,1,384]{2,1,0:T(1,128)S(1)} %all_to_all.11.got, f32[128,2048]{1,0:T(8,128)S(1)} %bitcast.7, f32[1,128]{1,0:T(1,128)S(1)} %shard_map.117.refs_3_.d.disp, f32[512,256]{1,0:T(8,128)S(1)} %get-tuple-element.53.refs_1_.r, f32[512,256]{1,0:T(8,128)S(1)} %get-tuple-element.61.v), custom_call_target="tpu_custom_call" | custom-call | tf_op jit(solution)/shard_map/final/pallas_call | solution.py:478
  (1 shorter events, 0.0 us)
Async XLA Ops:
  2.2 12.6 %collective-permute-start.4 = (f32[192,256]{1,0:T(8,128)S(1)}, f32[192,256]{1,0:T(8,128)S(1)}, u32[]{:S(2)}, u32[]{:S(2)}) collective-permute-start(f32[192,256]{1,0:T(8,128)S(1)} %get-tuple-element.50), channel_id=1, source_target_pairs={{0,16},{16,0},{32,48},{48,32},{64,80},{80,64},{96,112},{112,96},{1... | collective-permute-start | bytes 589832 | tf_op jit(solution)/shard_map/ppermute | solution.py:420
  3.7 11.1 %collective-permute-start.5 = (f32[192,256]{1,0:T(8,128)S(1)}, f32[192,256]{1,0:T(8,128)S(1)}, u32[]{:S(2)}, u32[]{:S(2)}) collective-permute-start(f32[192,256]{1,0:T(8,128)S(1)} %get-tuple-element.51), channel_id=1, source_target_pairs={{16,32},{32,16},{48,64},{64,48},{80,96},{96,80},{112,0},{0,112},{1... | collective-permute-start | bytes 589832 | tf_op jit(solution)/shard_map/ppermute | solution.py:419
  5.4 2.6 %collective-permute-start = (f32[32,128]{1,0:T(8,128)S(1)}, f32[32,128]{1,0:T(8,128)S(1)}, u32[]{:S(2)}, u32[]{:S(2)}) collective-permute-start(f32[32,128]{1,0:T(8,128)S(1)} %get-tuple-element.45), channel_id=1, source_target_pairs={{0,1},{1,0},{2,3},{3,2},{4,5},{5,4},{6,7},{7,6},{8,9},{9,8},{10,11... | collective-permute-start | bytes 49160 | tf_op jit(solution)/shard_map/ppermute | solution.py:420
  6.6 1.4 %collective-permute-start.1 = (f32[32,128]{1,0:T(8,128)S(1)}, f32[32,128]{1,0:T(8,128)S(1)}, u32[]{:S(2)}, u32[]{:S(2)}) collective-permute-start(f32[32,128]{1,0:T(8,128)S(1)} %get-tuple-element.45), channel_id=1, source_target_pairs={{1,2},{2,1},{3,4},{4,3},{5,6},{6,5},{7,8},{8,7},{9,10},{10,9},{11,... | collective-permute-start | bytes 49160 | tf_op jit(solution)/shard_map/ppermute | solution.py:419
  8.1 5.5 %collective-permute-start.2 = (f32[8,128]{1,0:T(8,128)S(1)}, f32[8,128]{1,0:T(8,128)S(1)}, u32[]{:S(2)}, u32[]{:S(2)}) collective-permute-start(f32[8,128]{1,0:T(8,128)S(1)} %get-tuple-element.48), channel_id=1, source_target_pairs={{0,16},{16,0},{32,48},{48,32},{64,80},{80,64},{96,112},{112,96},{1... | collective-permute-start | bytes 12296 | tf_op jit(solution)/shard_map/ppermute | solution.py:420
  11.8 3.0 %collective-permute-start.3 = (f32[8,128]{1,0:T(8,128)S(1)}, f32[8,128]{1,0:T(8,128)S(1)}, u32[]{:S(2)}, u32[]{:S(2)}) collective-permute-start(f32[8,128]{1,0:T(8,128)S(1)} %get-tuple-element.49), channel_id=1, source_target_pairs={{16,32},{32,16},{48,64},{64,48},{80,96},{96,80},{112,0},{0,112},{1... | collective-permute-start | bytes 12296 | tf_op jit(solution)/shard_map/ppermute | solution.py:419
  14.8 24.5 %copy-start = (f32[1,128,2048]{2,1,0:T(8,128)S(1)}, f32[1,128,2048]{2,1,0:T(8,128)}, u32[]{:S(2)}) copy-start(f32[1,128,2048]{2,1,0:T(8,128)} %param.18) | copy-start | bytes 3145732
  39.6 2.5 %collective-permute-start.6 = (f32[1,128]{1,0:T(1,128)S(1)}, f32[1,128]{1,0:T(1,128)S(1)}, u32[]{:S(2)}, u32[]{:S(2)}) collective-permute-start(f32[1,128]{1,0:T(1,128)S(1)} %shard_map.117.refs_3_.d.disp), channel_id=1, source_target_pairs={{0,1},{1,0},{2,3},{3,2},{4,5},{5,4},{6,7},{7,6},{8,9},{9,8},{10,11... | collective-permute-start | bytes 1544 | tf_op jit(solution)/shard_map/ppermute | solution.py:420
  40.0 2.1 %collective-permute-start.7 = (f32[1,128]{1,0:T(1,128)S(1)}, f32[1,128]{1,0:T(1,128)S(1)}, u32[]{:S(2)}, u32[]{:S(2)}) collective-permute-start(f32[1,128]{1,0:T(1,128)S(1)} %shard_map.117.refs_3_.d.disp), channel_id=1, source_target_pairs={{1,2},{2,1},{3,4},{4,3},{5,6},{6,5},{7,8},{8,7},{9,10},{10,9},{11,... | collective-permute-start | bytes 1544 | tf_op jit(solution)/shard_map/ppermute | solution.py:419
  42.1 4.2 %collective-permute-start.8 = (f32[3,128]{1,0:T(4,128)S(1)}, f32[3,128]{1,0:T(4,128)S(1)}, u32[]{:S(2)}, u32[]{:S(2)}) collective-permute-start(f32[3,128]{1,0:T(4,128)S(1)} %shard_map.120), channel_id=1, source_target_pairs={{0,16},{16,0},{32,48},{48,32},{64,80},{80,64},{96,112},{112,96},{1... | collective-permute-start | bytes 4616 | tf_op jit(solution)/shard_map/ppermute | solution.py:420
  44.0 3.0 %collective-permute-start.9 = (f32[3,128]{1,0:T(4,128)S(1)}, f32[3,128]{1,0:T(4,128)S(1)}, u32[]{:S(2)}, u32[]{:S(2)}) collective-permute-start(f32[3,128]{1,0:T(4,128)S(1)} %shard_map.120), channel_id=1, source_target_pairs={{16,32},{32,16},{48,64},{64,48},{80,96},{96,80},{112,0},{0,112},{1... | collective-permute-start | bytes 4616 | tf_op jit(solution)/shard_map/ppermute | solution.py:419
where the time goes:
time: 68.9 us; the launch traced here: 68.7 us
  blocking collectives  41.5 us (60%)
  starting transfers between devices  12.2 us (18%)
  Pallas kernels  10.1 us (15%)
  waiting for transfers between devices  4.13 us (6%)
  between operations  0.74 us (1%)
    all_to_all x2, blocking collectives, body(): got = lax.all_to_all(sent, AXES, 0, 0, tiled=True)  41.5 us
    ppermute x5, starting transfers between devices, trade(): near = lax.ppermute(a, axis, first)  8.65 us
    pallas_call x9, Pallas kernels, call(): pl.pallas_call(kernel, out_shape=[pltpu.VMEM(*o) for o in outs], in_specs...  7.27 us
    ppermute x5, starting transfers between devices, trade(): far = lax.ppermute(b, axis, second)  3.56 us
    ppermute x5, waiting for transfers between devices, trade(): near = lax.ppermute(a, axis, first)  2.18 us
    ppermute x5, waiting for transfers between devices, trade(): far = lax.ppermute(b, axis, second)  1.96 us
    pallas_call x1, Pallas kernels, body(): pl.pallas_call(pack, out_shape=[pltpu.VMEM((32, 128), f32)] + [pltpu.VMEM...  1.58 us
  transfers between devices with their start and end apart: 10, of which 4 were waited for; matrix products, arithmetic and copies ran while one was open for 0% of the time, Pallas kernels for 5%

commit v1 on v0

--- a/solution.py
+++ b/solution.py
@@ -383,7 +383,9 @@
     a, b = solve(got)
     displace(a, b, got, compliance, disp, out)
     for s in range(ES):
-        fluid[:, s, :] = a * r[at(s), :] + b * v[at(s), :]
+        field = a * r[at(s), :] + b * v[at(s), :]
+        for h in (0, 1):
+            fluid[pl.ds(h * ES + s, NODES, stride=2 * ES), :] = field[:, h * 128 : (h + 1) * 128]
 
 
 def call(kernel, outs, ins, scratch=()):
@@ -477,13 +479,14 @@
     near = pl.BlockSpec(memory_space=pltpu.VMEM)
     fluid, disp = pl.pallas_call(
         final_kernel,
-        out_shape=[jax.ShapeDtypeStruct((NODES, ES, EX), f32), jax.ShapeDtypeStruct(*row)],
+        out_shape=[jax.ShapeDtypeStruct((2 * ES * NODES, 128), f32), jax.ShapeDtypeStruct(*row)],
         in_specs=[near] * 5,
         out_specs=[near] * 2,
         compiler_params=pltpu.CompilerParams(vmem_limit_bytes=16 << 20),
         name="final",
     )(*(pltpu.with_memory_space_constraint(x, pltpu.VMEM) for x in (got, rows, disp, r, v)))
-    return fluid, disp[None]
+    fluid = fluid.reshape(NODES, 2, ES, 128).transpose(0, 2, 1, 3)
+    return fluid.reshape(source.shape), disp[None]
 
 
 def solution(mesh):

time: 68.9 us -> 68.9 us (level)
  no operation moved by 1% of the time
where the time goes in v1:
time: 68.9 us; the launch traced here: 68.7 us
  blocking collectives  41.5 us (60%)
  starting transfers between devices  12.2 us (18%)
  Pallas kernels  10.1 us (15%)
  waiting for transfers between devices  4.13 us (6%)
  between operations  0.74 us (1%)
    all_to_all x2, blocking collectives, body(): got = lax.all_to_all(sent, AXES, 0, 0, tiled=True)  41.5 us
    ppermute x5, starting transfers between devices, trade(): near = lax.ppermute(a, axis, first)  8.65 us
    pallas_call x9, Pallas kernels, call(): pl.pallas_call(kernel, out_shape=[pltpu.VMEM(*o) for o in outs], in_specs...  7.27 us
    ppermute x5, starting transfers between devices, trade(): far = lax.ppermute(b, axis, second)  3.56 us
    ppermute x5, waiting for transfers between devices, trade(): near = lax.ppermute(a, axis, first)  2.18 us
    ppermute x5, waiting for transfers between devices, trade(): far = lax.ppermute(b, axis, second)  1.96 us
    pallas_call x1, Pallas kernels, body(): pl.pallas_call(pack, out_shape=[pltpu.VMEM((32, 128), f32)] + [pltpu.VMEM...  1.58 us
  transfers between devices with their start and end apart: 10, of which 4 were waited for; matrix products, arithmetic and copies ran while one was open for 0% of the time, Pallas kernels for 5%

profile of v1, /device:TPU:1, one launch (start us, length us, event | category | flops | bytes accessed | tf_op | source)
XLA Modules:
  0.0 68.7 jit_solution(3482049457495562422)
XLA Ops:
  0.6 1.6 %pack.1 = (f32[32,128]{1,0:T(8,128)S(1)}, f32[192,256]{1,0:T(8,128)S(1)}, f32[192,256]{1,0:T(8,128)S(1)}, f32[512,256]{1,0:T(8,128)S(1)}, f32[512,256]{1,0:T(8,1...) custom-call(f32[512,256]{1,0:T(8,128)} %bitcast.13, ...), custom_call_target="tpu_custom_call" | custom-call | tf_op jit(solution)/shard_map/pack/pallas_call | solution.py:427
  2.2 1.4 %collective-permute-start.4 = (f32[192,256]{1,0:T(8,128)S(1)}, f32[192,256]{1,0:T(8,128)S(1)}, u32[]{:S(2)}, u32[]{:S(2)}) collective-permute-start(f32[192,256]{1,0:T(8,128)S(1)} %get-tuple-element.50), channel_id=1, source_target_pairs={{0,16},{16,0},{32,48},{48,32},{64,80},{80,64},{96,112},{112,96},{1... | collective-permute-start | bytes 589832 | tf_op jit(solution)/shard_map/ppermute | solution.py:422
  3.7 1.7 %collective-permute-start.5 = (f32[192,256]{1,0:T(8,128)S(1)}, f32[192,256]{1,0:T(8,128)S(1)}, u32[]{:S(2)}, u32[]{:S(2)}) collective-permute-start(f32[192,256]{1,0:T(8,128)S(1)} %get-tuple-element.51), channel_id=1, source_target_pairs={{16,32},{32,16},{48,64},{64,48},{80,96},{96,80},{112,0},{0,112},{1... | collective-permute-start | bytes 589832 | tf_op jit(solution)/shard_map/ppermute | solution.py:421
  5.4 1.2 %collective-permute-start = (f32[32,128]{1,0:T(8,128)S(1)}, f32[32,128]{1,0:T(8,128)S(1)}, u32[]{:S(2)}, u32[]{:S(2)}) collective-permute-start(f32[32,128]{1,0:T(8,128)S(1)} %get-tuple-element.45), channel_id=1, source_target_pairs={{0,1},{1,0},{2,3},{3,2},{4,5},{5,4},{6,7},{7,6},{8,9},{9,8},{10,11... | collective-permute-start | bytes 49160 | tf_op jit(solution)/shard_map/ppermute | solution.py:422
  6.6 0.7 collective-permute-start.1
  7.3 0.7 %collective-permute-done.refs_2_.cross_a = f32[32,128]{1,0:T(8,128)S(1)} collective-permute-done((f32[32,128]{1,0:T(8,128)S(1)}, f32[32,128]{1,0:T(8,128)S(1)}, u32[]{:S(2)}, u32[]{:S(2)}) %collective-permute-start) | collective-permute-done | bytes 16416 | tf_op jit(solution)/shard_map/ppermute | solution.py:422
  8.0 0.0 collective-permute-done.1.refs_3_.cross_b
  8.0 0.1 shard_map.115
  8.1 3.7 %collective-permute-start.2 = (f32[8,128]{1,0:T(8,128)S(1)}, f32[8,128]{1,0:T(8,128)S(1)}, u32[]{:S(2)}, u32[]{:S(2)}) collective-permute-start(f32[8,128]{1,0:T(8,128)S(1)} %get-tuple-element.48), channel_id=1, source_target_pairs={{0,16},{16,0},{32,48},{48,32},{64,80},{80,64},{96,112},{112,96},{1... | collective-permute-start | bytes 12296 | tf_op jit(solution)/shard_map/ppermute | solution.py:422
  11.8 0.0 collective-permute-start.3
  11.8 1.1 %shard_map.113 = (f32[512,256]{1,0:T(8,128)S(1)}, f32[640,384]{1,0:T(8,128)S(1)}, f32[1,128]{1,0:T(1,128)S(1)}, bf16[320,192]{1,0:T(8,128)(2,1)S(1)}) custom-call(f32[512,256]{1,0:T(8,128)S(1)} %get-tuple-element.34.refs_0_, f32[512,256]{1,0:T(8,128)S(1)} %get-tuple-element.33.refs_1_.refs_0_, s32[1,128]{1,0:T(1,128)S(1)} %get-tuple-element.35.refs_2_.own.refs_7_, ...), custom_call_target="tpu_custom_call" | custom-call | tf_op jit(solution)/shard_map/pallas_call | solution.py:393
  12.9 0.7 shard_map.114
  13.5 0.0 collective-permute-done.2.refs_5_
  13.6 1.3 %collective-permute-done.3.refs_6_ = f32[8,128]{1,0:T(8,128)S(1)} collective-permute-done((f32[8,128]{1,0:T(8,128)S(1)}, f32[8,128]{1,0:T(8,128)S(1)}, u32[]{:S(2)}, u32[]{:S(2)}) %collective-permute-start.3) | collective-permute-done | bytes 4128 | tf_op jit(solution)/shard_map/ppermute | solution.py:421
  14.8 0.0 collective-permute-done.4.refs_8_
  14.8 0.0 collective-permute-done.5.refs_9_
  14.8 0.0 copy-start
  14.8 1.7 %shard_map.116 = (f32[128,1,384]{2,1,0:T(1,128)S(1)}, f32[384,256]{1,0:T(8,128)S(1)}, f32[128,128]{1,0:T(8,128)S(1)}) custom-call(f32[512,256]{1,0:T(8,128)S(1)} %get-tuple-element.33.refs_1_.refs_0_, f32[512,256]{1,0:T(8,128)S(1)} %get-tuple-element.42.refs_1_, f32[640,384]{1,0:T(8,128)S(1)} %get-tuple-element.46.refs_2_, ...), custom_call_target="tpu_custom_call" | custom-call | tf_op jit(solution)/shard_map/pallas_call | solution.py:393
  16.5 22.8 %all_to_all.10.got = f32[128,1,384]{2,1,0:T(1,128)S(1)} all-to-all(f32[128,1,384]{2,1,0:T(1,128)S(1)} %get-tuple-element.52), channel_id=1, replica_groups=mesh['span'=8,'xs'=16] {'span','xs'}, dimensions={0} | all-to-all | bytes 393216 | tf_op jit(solution)/shard_map/all_to_all | solution.py:461
  39.3 0.0 copy-done
  39.3 0.3 shard_map.117.refs_3_.d.disp
  39.6 0.4 collective-permute-start.6
  40.0 0.6 collective-permute-start.7
  40.7 1.5 %collective-permute-done.6.refs_4_.cross_a = f32[1,128]{1,0:T(1,128)S(1)} collective-permute-done((f32[1,128]{1,0:T(1,128)S(1)}, f32[1,128]{1,0:T(1,128)S(1)}, u32[]{:S(2)}, u32[]{:S(2)}) %collective-permute-start.6) | collective-permute-done | bytes 544 | tf_op jit(solution)/shard_map/ppermute | solution.py:422
  42.1 0.0 collective-permute-done.7.refs_5_.cross_b
  42.1 1.9 %collective-permute-start.8 = (f32[3,128]{1,0:T(4,128)S(1)}, f32[3,128]{1,0:T(4,128)S(1)}, u32[]{:S(2)}, u32[]{:S(2)}) collective-permute-start(f32[3,128]{1,0:T(4,128)S(1)} %shard_map.120), channel_id=1, source_target_pairs={{0,16},{16,0},{32,48},{48,32},{64,80},{80,64},{96,112},{112,96},{1... | collective-permute-start | bytes 4616 | tf_op jit(solution)/shard_map/ppermute | solution.py:422
  44.0 0.5 collective-permute-start.9
  44.6 1.1 %shard_map.118 = (f32[512,256]{1,0:T(8,128)S(1)}, f32[640,384]{1,0:T(8,128)S(1)}, f32[1,128]{1,0:T(1,128)S(1)}) custom-call(f32[512,256]{1,0:T(8,128)S(1)} %get-tuple-element.34.refs_0_, f32[512,256]{1,0:T(8,128)S(1)} %get-tuple-element.33.refs_1_.refs_0_, s32[1,128]{1,0:T(1,128)S(1)} %get-tuple-element.35.refs_2_.own.refs_7_, ...), custom_call_target="tpu_custom_call" | custom-call | tf_op jit(solution)/shard_map/pallas_call | solution.py:393
  45.7 0.7 shard_map.119.refs_2_
  46.3 0.0 collective-permute-done.8.refs_8_
  46.3 0.7 %collective-permute-done.9.refs_9_ = f32[3,128]{1,0:T(4,128)S(1)} collective-permute-done((f32[3,128]{1,0:T(4,128)S(1)}, f32[3,128]{1,0:T(4,128)S(1)}, u32[]{:S(2)}, u32[]{:S(2)}) %collective-permute-start.9) | collective-permute-done | bytes 1568 | tf_op jit(solution)/shard_map/ppermute | solution.py:421
  47.0 1.6 %shard_map.121 = (f32[128,1,384]{2,1,0:T(1,128)S(1)}, f32[512,256]{1,0:T(8,128)S(1)}) custom-call(f32[512,256]{1,0:T(8,128)S(1)} %get-tuple-element.33.refs_1_.refs_0_, f32[512,256]{1,0:T(8,128)S(1)} %get-tuple-element.53.refs_1_.r, f32[640,384]{1,0:T(8,128)S(1)} %shard_map.119.refs_2_, f32[1,128]{1,0:T(1,128)S(1)} %get-tuple-element.57.refs_3_, ...), custom_call_target="tpu_custom_call" | custom-call | tf_op jit(solution)/shard_map/pallas_call | solution.py:393
  48.7 18.8 %all_to_all.11.got = f32[128,1,384]{2,1,0:T(1,128)S(1)} all-to-all(f32[128,1,384]{2,1,0:T(1,128)S(1)} %get-tuple-element.60), channel_id=1, replica_groups=mesh['span'=8,'xs'=16] {'span','xs'}, dimensions={0} | all-to-all | bytes 393216 | tf_op jit(solution)/shard_map/all_to_all | solution.py:478
  67.5 1.2 %final.1 = (f32[1024,128]{1,0:T(8,128)}, f32[1,128]{1,0:T(1,128)}) custom-call(f32[128,1,384]{2,1,0:T(1,128)S(1)} %all_to_all.11.got, f32[128,2048]{1,0:T(8,128)S(1)} %bitcast.12, f32[1,128]{1,0:T(1,128)S(1)} %shard_map.117.refs_3_.d.disp, f32[512,256]{1,0:T(8,128)S(1)} %get-tuple-element.53.refs_1_.r, f32[512,256]{1,0:T(8,128)S(1)} %get-tuple-element.61.v), custom_call_target="tpu_custom_call" | custom-call | tf_op jit(solution)/shard_map/final/pallas_call | solution.py:480
  (1 shorter events, 0.0 us)
Async XLA Ops:
  2.2 12.6 %collective-permute-start.4 = (f32[192,256]{1,0:T(8,128)S(1)}, f32[192,256]{1,0:T(8,128)S(1)}, u32[]{:S(2)}, u32[]{:S(2)}) collective-permute-start(f32[192,256]{1,0:T(8,128)S(1)} %get-tuple-element.50), channel_id=1, source_target_pairs={{0,16},{16,0},{32,48},{48,32},{64,80},{80,64},{96,112},{112,96},{1... | collective-permute-start | bytes 589832 | tf_op jit(solution)/shard_map/ppermute | solution.py:422
  3.7 11.1 %collective-permute-start.5 = (f32[192,256]{1,0:T(8,128)S(1)}, f32[192,256]{1,0:T(8,128)S(1)}, u32[]{:S(2)}, u32[]{:S(2)}) collective-permute-start(f32[192,256]{1,0:T(8,128)S(1)} %get-tuple-element.51), channel_id=1, source_target_pairs={{16,32},{32,16},{48,64},{64,48},{80,96},{96,80},{112,0},{0,112},{1... | collective-permute-start | bytes 589832 | tf_op jit(solution)/shard_map/ppermute | solution.py:421
  5.4 2.6 %collective-permute-start = (f32[32,128]{1,0:T(8,128)S(1)}, f32[32,128]{1,0:T(8,128)S(1)}, u32[]{:S(2)}, u32[]{:S(2)}) collective-permute-start(f32[32,128]{1,0:T(8,128)S(1)} %get-tuple-element.45), channel_id=1, source_target_pairs={{0,1},{1,0},{2,3},{3,2},{4,5},{5,4},{6,7},{7,6},{8,9},{9,8},{10,11... | collective-permute-start | bytes 49160 | tf_op jit(solution)/shard_map/ppermute | solution.py:422
  6.6 1.4 %collective-permute-start.1 = (f32[32,128]{1,0:T(8,128)S(1)}, f32[32,128]{1,0:T(8,128)S(1)}, u32[]{:S(2)}, u32[]{:S(2)}) collective-permute-start(f32[32,128]{1,0:T(8,128)S(1)} %get-tuple-element.45), channel_id=1, source_target_pairs={{1,2},{2,1},{3,4},{4,3},{5,6},{6,5},{7,8},{8,7},{9,10},{10,9},{11,... | collective-permute-start | bytes 49160 | tf_op jit(solution)/shard_map/ppermute | solution.py:421
  8.1 5.5 %collective-permute-start.2 = (f32[8,128]{1,0:T(8,128)S(1)}, f32[8,128]{1,0:T(8,128)S(1)}, u32[]{:S(2)}, u32[]{:S(2)}) collective-permute-start(f32[8,128]{1,0:T(8,128)S(1)} %get-tuple-element.48), channel_id=1, source_target_pairs={{0,16},{16,0},{32,48},{48,32},{64,80},{80,64},{96,112},{112,96},{1... | collective-permute-start | bytes 12296 | tf_op jit(solution)/shard_map/ppermute | solution.py:422
  11.8 3.0 %collective-permute-start.3 = (f32[8,128]{1,0:T(8,128)S(1)}, f32[8,128]{1,0:T(8,128)S(1)}, u32[]{:S(2)}, u32[]{:S(2)}) collective-permute-start(f32[8,128]{1,0:T(8,128)S(1)} %get-tuple-element.49), channel_id=1, source_target_pairs={{16,32},{32,16},{48,64},{64,48},{80,96},{96,80},{112,0},{0,112},{1... | collective-permute-start | bytes 12296 | tf_op jit(solution)/shard_map/ppermute | solution.py:421
  14.8 24.5 %copy-start = (f32[1,128,2048]{2,1,0:T(8,128)S(1)}, f32[1,128,2048]{2,1,0:T(8,128)}, u32[]{:S(2)}) copy-start(f32[1,128,2048]{2,1,0:T(8,128)} %param.18) | copy-start | bytes 3145732
  39.6 2.5 %collective-permute-start.6 = (f32[1,128]{1,0:T(1,128)S(1)}, f32[1,128]{1,0:T(1,128)S(1)}, u32[]{:S(2)}, u32[]{:S(2)}) collective-permute-start(f32[1,128]{1,0:T(1,128)S(1)} %shard_map.117.refs_3_.d.disp), channel_id=1, source_target_pairs={{0,1},{1,0},{2,3},{3,2},{4,5},{5,4},{6,7},{7,6},{8,9},{9,8},{10,11... | collective-permute-start | bytes 1544 | tf_op jit(solution)/shard_map/ppermute | solution.py:422
  40.0 2.1 %collective-permute-start.7 = (f32[1,128]{1,0:T(1,128)S(1)}, f32[1,128]{1,0:T(1,128)S(1)}, u32[]{:S(2)}, u32[]{:S(2)}) collective-permute-start(f32[1,128]{1,0:T(1,128)S(1)} %shard_map.117.refs_3_.d.disp), channel_id=1, source_target_pairs={{1,2},{2,1},{3,4},{4,3},{5,6},{6,5},{7,8},{8,7},{9,10},{10,9},{11,... | collective-permute-start | bytes 1544 | tf_op jit(solution)/shard_map/ppermute | solution.py:421
  42.1 4.2 %collective-permute-start.8 = (f32[3,128]{1,0:T(4,128)S(1)}, f32[3,128]{1,0:T(4,128)S(1)}, u32[]{:S(2)}, u32[]{:S(2)}) collective-permute-start(f32[3,128]{1,0:T(4,128)S(1)} %shard_map.120), channel_id=1, source_target_pairs={{0,16},{16,0},{32,48},{48,32},{64,80},{80,64},{96,112},{112,96},{1... | collective-permute-start | bytes 4616 | tf_op jit(solution)/shard_map/ppermute | solution.py:422
  44.0 3.0 %collective-permute-start.9 = (f32[3,128]{1,0:T(4,128)S(1)}, f32[3,128]{1,0:T(4,128)S(1)}, u32[]{:S(2)}, u32[]{:S(2)}) collective-permute-start(f32[3,128]{1,0:T(4,128)S(1)} %shard_map.120), channel_id=1, source_target_pairs={{16,32},{32,16},{48,64},{64,48},{80,96},{96,80},{112,0},{0,112},{1... | collective-permute-start | bytes 4616 | tf_op jit(solution)/shard_map/ppermute | solution.py:421

commit v2 on v1

--- a/solution.py
+++ b/solution.py
@@ -348,13 +348,13 @@
         gram = gram + jnp.where(lane == k, total, 0.0)
     v_mid = v_scr[NODES : 9 * NODES, :EX]
     rows = [gram, tr[...], trace(v_mid, spot)]
-    msg[...] = jnp.broadcast_to(jnp.concatenate(rows, 1)[None], msg.shape)
+    msg[...] = jnp.concatenate(rows * 128, 0)
     if not first:
         v_out[...] = v_mid
 
 
 def solve(got):
-    total = jnp.sum(got[:, 0, :128], axis=0, keepdims=True)
+    total = jnp.sum(got[pl.ds(0, 128, stride=3), :], axis=0, keepdims=True)
     lane = lax.broadcasted_iota(jnp.int32, (1, 128), 1)
     g11, g12, g22, g1, g2 = (
         jnp.sum(jnp.where(lane == k, total, 0.0), axis=1, keepdims=True) for k in range(5)
@@ -366,8 +366,8 @@
 
 
 def displace(a, b, got, compliance, disp, out):
-    start = position()[0] * 16
-    traces = a * got[pl.ds(start, 16), 0, 128:256] + b * got[pl.ds(start, 16), 0, 256:]
+    start = position()[0] * 48
+    traces = a * got[pl.ds(start + 1, 16, stride=3), :] + b * got[pl.ds(start + 2, 16, stride=3), :]
     acc = jnp.zeros((IFN, 128), f32)
     for j in range(16):
         acc = acc + compliance[:, j * 128 : (j + 1) * 128] * traces[j : j + 1]
@@ -413,7 +413,7 @@
     n_xs = lax.axis_size("xs")
     own, disp, rows = interface[0], start_displacement[0], compliance[0]
     mats = [volume_matrix, span_lower, span_upper, cross_lower, cross_upper]
-    message, block = ((128, 1, 3 * 128), f32), ((ES * NODES, EX), f32)
+    message, block = ((3 * 128, 128), f32), ((ES * NODES, EX), f32)
     row, wide = ((1, 128), f32), ((10 * NODES, LANES), f32)
 
     def trade(axis, a, b):
@@ -458,7 +458,7 @@
         [message, ((6 * NODES, EX), f32), ((2 * NODES, 128), f32)],
         [cf, r, part, tr, split, *around, *ends], scratch,
     )
-    got = lax.all_to_all(sent, AXES, 0, 0, tiled=True)
+    got = lax.all_to_all(sent.reshape(128, 1, 384), AXES, 0, 0, tiled=True).reshape(384, 128)
     (disp,) = call(shell_kernel, [row], [got, rows, disp])
     beside = trade("xs", disp, disp)
     r, part, tr = call(
@@ -475,7 +475,7 @@
         lambda *refs: outer_kernel(False, n_xs, *refs), [message, block],
         [cf, r, part, tr, split, *around, *over, *static], scratch,
     )
-    got = lax.all_to_all(sent, AXES, 0, 0, tiled=True)
+    got = lax.all_to_all(sent.reshape(128, 1, 384), AXES, 0, 0, tiled=True).reshape(384, 128)
     near = pl.BlockSpec(memory_space=pltpu.VMEM)
     fluid, disp = pl.pallas_call(
         final_kernel,

time: 68.9 us -> 68.8 us (level)
  no operation moved by 1% of the time
where the time goes in v2:
time: 68.8 us; the launch traced here: 68.6 us
  blocking collectives  41.5 us (60%)
  starting transfers between devices  12.2 us (18%)
  Pallas kernels  9.95 us (14%)
  waiting for transfers between devices  4.13 us (6%)
  between operations  0.74 us (1%)
    all_to_all x2, blocking collectives, body(): lax.all_to_all(sent.reshape(128, 1, 384), AXES, 0, 0, tiled=True)  41.5 us
    ppermute x5, starting transfers between devices, trade(): near = lax.ppermute(a, axis, first)  8.65 us
    pallas_call x9, Pallas kernels, call(): pl.pallas_call(kernel, out_shape=[pltpu.VMEM(*o) for o in outs], in_specs...  7.18 us
    ppermute x5, starting transfers between devices, trade(): far = lax.ppermute(b, axis, second)  3.56 us
    ppermute x5, waiting for transfers between devices, trade(): near = lax.ppermute(a, axis, first)  2.18 us
    ppermute x5, waiting for transfers between devices, trade(): far = lax.ppermute(b, axis, second)  1.95 us
    pallas_call x1, Pallas kernels, body(): pl.pallas_call(pack, out_shape=[pltpu.VMEM((32, 128), f32)] + [pltpu.VMEM...  1.58 us
  transfers between devices with their start and end apart: 10, of which 4 were waited for; matrix products, arithmetic and copies ran while one was open for 0% of the time, Pallas kernels for 5%

profile of v2, /device:TPU:1, one launch (start us, length us, event | category | flops | bytes accessed | tf_op | source)
XLA Modules:
  0.0 68.6 jit_solution(13406257992683806676)
XLA Ops:
  0.6 1.6 %pack.1 = (f32[32,128]{1,0:T(8,128)S(1)}, f32[192,256]{1,0:T(8,128)S(1)}, f32[192,256]{1,0:T(8,128)S(1)}, f32[512,256]{1,0:T(8,128)S(1)}, f32[512,256]{1,0:T(8,1...) custom-call(f32[512,256]{1,0:T(8,128)} %bitcast.21, ...), custom_call_target="tpu_custom_call" | custom-call | tf_op jit(solution)/shard_map/pack/pallas_call | solution.py:427
  2.2 1.4 %collective-permute-start.4 = (f32[192,256]{1,0:T(8,128)S(1)}, f32[192,256]{1,0:T(8,128)S(1)}, u32[]{:S(2)}, u32[]{:S(2)}) collective-permute-start(f32[192,256]{1,0:T(8,128)S(1)} %get-tuple-element.50), channel_id=1, source_target_pairs={{0,16},{16,0},{32,48},{48,32},{64,80},{80,64},{96,112},{112,96},{1... | collective-permute-start | bytes 589832 | tf_op jit(solution)/shard_map/ppermute | solution.py:422
  3.7 1.7 %collective-permute-start.5 = (f32[192,256]{1,0:T(8,128)S(1)}, f32[192,256]{1,0:T(8,128)S(1)}, u32[]{:S(2)}, u32[]{:S(2)}) collective-permute-start(f32[192,256]{1,0:T(8,128)S(1)} %get-tuple-element.51), channel_id=1, source_target_pairs={{16,32},{32,16},{48,64},{64,48},{80,96},{96,80},{112,0},{0,112},{1... | collective-permute-start | bytes 589832 | tf_op jit(solution)/shard_map/ppermute | solution.py:421
  5.4 1.2 %collective-permute-start = (f32[32,128]{1,0:T(8,128)S(1)}, f32[32,128]{1,0:T(8,128)S(1)}, u32[]{:S(2)}, u32[]{:S(2)}) collective-permute-start(f32[32,128]{1,0:T(8,128)S(1)} %get-tuple-element.45), channel_id=1, source_target_pairs={{0,1},{1,0},{2,3},{3,2},{4,5},{5,4},{6,7},{7,6},{8,9},{9,8},{10,11... | collective-permute-start | bytes 49160 | tf_op jit(solution)/shard_map/ppermute | solution.py:422
  6.6 0.7 collective-permute-start.1
  7.3 0.7 %collective-permute-done.refs_2_.cross_a = f32[32,128]{1,0:T(8,128)S(1)} collective-permute-done((f32[32,128]{1,0:T(8,128)S(1)}, f32[32,128]{1,0:T(8,128)S(1)}, u32[]{:S(2)}, u32[]{:S(2)}) %collective-permute-start) | collective-permute-done | bytes 16416 | tf_op jit(solution)/shard_map/ppermute | solution.py:422
  8.0 0.0 collective-permute-done.1.refs_3_.cross_b
  8.0 0.1 shard_map.115
  8.1 3.7 %collective-permute-start.2 = (f32[8,128]{1,0:T(8,128)S(1)}, f32[8,128]{1,0:T(8,128)S(1)}, u32[]{:S(2)}, u32[]{:S(2)}) collective-permute-start(f32[8,128]{1,0:T(8,128)S(1)} %get-tuple-element.48), channel_id=1, source_target_pairs={{0,16},{16,0},{32,48},{48,32},{64,80},{80,64},{96,112},{112,96},{1... | collective-permute-start | bytes 12296 | tf_op jit(solution)/shard_map/ppermute | solution.py:422
  11.8 0.0 collective-permute-start.3
  11.8 1.1 %shard_map.113 = (f32[512,256]{1,0:T(8,128)S(1)}, f32[640,384]{1,0:T(8,128)S(1)}, f32[1,128]{1,0:T(1,128)S(1)}, bf16[320,192]{1,0:T(8,128)(2,1)S(1)}) custom-call(f32[512,256]{1,0:T(8,128)S(1)} %get-tuple-element.34.refs_0_, f32[512,256]{1,0:T(8,128)S(1)} %get-tuple-element.33.refs_1_.refs_0_, s32[1,128]{1,0:T(1,128)S(1)} %get-tuple-element.35.refs_2_.own.refs_7_, ...), custom_call_target="tpu_custom_call" | custom-call | tf_op jit(solution)/shard_map/pallas_call | solution.py:393
  12.9 0.7 shard_map.114
  13.5 0.0 collective-permute-done.2.refs_5_
  13.6 1.3 %collective-permute-done.3.refs_6_ = f32[8,128]{1,0:T(8,128)S(1)} collective-permute-done((f32[8,128]{1,0:T(8,128)S(1)}, f32[8,128]{1,0:T(8,128)S(1)}, u32[]{:S(2)}, u32[]{:S(2)}) %collective-permute-start.3) | collective-permute-done | bytes 4128 | tf_op jit(solution)/shard_map/ppermute | solution.py:421
  14.8 0.0 collective-permute-done.4.refs_8_
  14.8 0.0 collective-permute-done.5.refs_9_
  14.8 0.0 copy-start
  14.8 1.7 %shard_map.116 = (f32[384,128]{1,0:T(8,128)S(1)}, f32[384,256]{1,0:T(8,128)S(1)}, f32[128,128]{1,0:T(8,128)S(1)}) custom-call(f32[512,256]{1,0:T(8,128)S(1)} %get-tuple-element.33.refs_1_.refs_0_, f32[512,256]{1,0:T(8,128)S(1)} %get-tuple-element.42.refs_1_, f32[640,384]{1,0:T(8,128)S(1)} %get-tuple-element.46.refs_2_, ...), custom_call_target="tpu_custom_call" | custom-call | tf_op jit(solution)/shard_map/pallas_call | solution.py:393
  16.5 22.8 %all_to_all.10 = f32[128,1,384]{2,1,0:T(1,128)S(1)} all-to-all(f32[128,1,384]{2,1,0:T(1,128)S(1)} %bitcast.20), channel_id=1, replica_groups=mesh['span'=8,'xs'=16] {'span','xs'}, dimensions={0} | all-to-all | bytes 393216 | tf_op jit(solution)/shard_map/all_to_all | solution.py:461
  39.3 0.0 copy-done
  39.3 0.3 shard_map.117.refs_3_.d.disp
  39.5 0.4 collective-permute-start.6
  39.9 0.6 collective-permute-start.7
  40.6 1.5 %collective-permute-done.6.refs_4_.cross_a = f32[1,128]{1,0:T(1,128)S(1)} collective-permute-done((f32[1,128]{1,0:T(1,128)S(1)}, f32[1,128]{1,0:T(1,128)S(1)}, u32[]{:S(2)}, u32[]{:S(2)}) %collective-permute-start.6) | collective-permute-done | bytes 544 | tf_op jit(solution)/shard_map/ppermute | solution.py:422
  42.0 0.0 collective-permute-done.7.refs_5_.cross_b
  42.1 1.9 %collective-permute-start.8 = (f32[3,128]{1,0:T(4,128)S(1)}, f32[3,128]{1,0:T(4,128)S(1)}, u32[]{:S(2)}, u32[]{:S(2)}) collective-permute-start(f32[3,128]{1,0:T(4,128)S(1)} %shard_map.120), channel_id=1, source_target_pairs={{0,16},{16,0},{32,48},{48,32},{64,80},{80,64},{96,112},{112,96},{1... | collective-permute-start | bytes 4616 | tf_op jit(solution)/shard_map/ppermute | solution.py:422
  44.0 0.5 collective-permute-start.9
  44.5 1.1 %shard_map.118 = (f32[512,256]{1,0:T(8,128)S(1)}, f32[640,384]{1,0:T(8,128)S(1)}, f32[1,128]{1,0:T(1,128)S(1)}) custom-call(f32[512,256]{1,0:T(8,128)S(1)} %get-tuple-element.34.refs_0_, f32[512,256]{1,0:T(8,128)S(1)} %get-tuple-element.33.refs_1_.refs_0_, s32[1,128]{1,0:T(1,128)S(1)} %get-tuple-element.35.refs_2_.own.refs_7_, ...), custom_call_target="tpu_custom_call" | custom-call | tf_op jit(solution)/shard_map/pallas_call | solution.py:393
  45.6 0.7 shard_map.119.refs_2_
  46.3 0.0 collective-permute-done.8.refs_8_
  46.3 0.7 %collective-permute-done.9.refs_9_ = f32[3,128]{1,0:T(4,128)S(1)} collective-permute-done((f32[3,128]{1,0:T(4,128)S(1)}, f32[3,128]{1,0:T(4,128)S(1)}, u32[]{:S(2)}, u32[]{:S(2)}) %collective-permute-start.9) | collective-permute-done | bytes 1568 | tf_op jit(solution)/shard_map/ppermute | solution.py:421
  47.0 1.6 %shard_map.121 = (f32[384,128]{1,0:T(8,128)S(1)}, f32[512,256]{1,0:T(8,128)S(1)}) custom-call(f32[512,256]{1,0:T(8,128)S(1)} %get-tuple-element.33.refs_1_.refs_0_, f32[512,256]{1,0:T(8,128)S(1)} %get-tuple-element.53.refs_1_.r, f32[640,384]{1,0:T(8,128)S(1)} %shard_map.119.refs_2_, f32[1,128]{1,0:T(1,128)S(1)} %get-tuple-element.57.refs_3_, ...), custom_call_target="tpu_custom_call" | custom-call | tf_op jit(solution)/shard_map/pallas_call | solution.py:393
  48.6 18.8 %all_to_all.11 = f32[128,1,384]{2,1,0:T(1,128)S(1)} all-to-all(f32[128,1,384]{2,1,0:T(1,128)S(1)} %bitcast.19), channel_id=1, replica_groups=mesh['span'=8,'xs'=16] {'span','xs'}, dimensions={0} | all-to-all | bytes 393216 | tf_op jit(solution)/shard_map/all_to_all | solution.py:478
  67.4 1.2 %final.1 = (f32[1024,128]{1,0:T(8,128)}, f32[1,128]{1,0:T(1,128)}) custom-call(f32[384,128]{1,0:T(8,128)S(1)} %bitcast.17, f32[128,2048]{1,0:T(8,128)S(1)} %bitcast.16, f32[1,128]{1,0:T(1,128)S(1)} %shard_map.117.refs_3_.d.disp, f32[512,256]{1,0:T(8,128)S(1)} %get-tuple-element.53.refs_1_.r, f32[512,256]{1,0:T(8,128)S(1)} %get-tuple-element.61.v), custom_call_target="tpu_custom_call" | custom-call | tf_op jit(solution)/shard_map/final/pallas_call | solution.py:480
  (1 shorter events, 0.0 us)
Async XLA Ops:
  2.2 12.6 %collective-permute-start.4 = (f32[192,256]{1,0:T(8,128)S(1)}, f32[192,256]{1,0:T(8,128)S(1)}, u32[]{:S(2)}, u32[]{:S(2)}) collective-permute-start(f32[192,256]{1,0:T(8,128)S(1)} %get-tuple-element.50), channel_id=1, source_target_pairs={{0,16},{16,0},{32,48},{48,32},{64,80},{80,64},{96,112},{112,96},{1... | collective-permute-start | bytes 589832 | tf_op jit(solution)/shard_map/ppermute | solution.py:422
  3.7 11.1 %collective-permute-start.5 = (f32[192,256]{1,0:T(8,128)S(1)}, f32[192,256]{1,0:T(8,128)S(1)}, u32[]{:S(2)}, u32[]{:S(2)}) collective-permute-start(f32[192,256]{1,0:T(8,128)S(1)} %get-tuple-element.51), channel_id=1, source_target_pairs={{16,32},{32,16},{48,64},{64,48},{80,96},{96,80},{112,0},{0,112},{1... | collective-permute-start | bytes 589832 | tf_op jit(solution)/shard_map/ppermute | solution.py:421
  5.4 2.6 %collective-permute-start = (f32[32,128]{1,0:T(8,128)S(1)}, f32[32,128]{1,0:T(8,128)S(1)}, u32[]{:S(2)}, u32[]{:S(2)}) collective-permute-start(f32[32,128]{1,0:T(8,128)S(1)} %get-tuple-element.45), channel_id=1, source_target_pairs={{0,1},{1,0},{2,3},{3,2},{4,5},{5,4},{6,7},{7,6},{8,9},{9,8},{10,11... | collective-permute-start | bytes 49160 | tf_op jit(solution)/shard_map/ppermute | solution.py:422
  6.6 1.4 %collective-permute-start.1 = (f32[32,128]{1,0:T(8,128)S(1)}, f32[32,128]{1,0:T(8,128)S(1)}, u32[]{:S(2)}, u32[]{:S(2)}) collective-permute-start(f32[32,128]{1,0:T(8,128)S(1)} %get-tuple-element.45), channel_id=1, source_target_pairs={{1,2},{2,1},{3,4},{4,3},{5,6},{6,5},{7,8},{8,7},{9,10},{10,9},{11,... | collective-permute-start | bytes 49160 | tf_op jit(solution)/shard_map/ppermute | solution.py:421
  8.1 5.5 %collective-permute-start.2 = (f32[8,128]{1,0:T(8,128)S(1)}, f32[8,128]{1,0:T(8,128)S(1)}, u32[]{:S(2)}, u32[]{:S(2)}) collective-permute-start(f32[8,128]{1,0:T(8,128)S(1)} %get-tuple-element.48), channel_id=1, source_target_pairs={{0,16},{16,0},{32,48},{48,32},{64,80},{80,64},{96,112},{112,96},{1... | collective-permute-start | bytes 12296 | tf_op jit(solution)/shard_map/ppermute | solution.py:422
  11.8 3.0 %collective-permute-start.3 = (f32[8,128]{1,0:T(8,128)S(1)}, f32[8,128]{1,0:T(8,128)S(1)}, u32[]{:S(2)}, u32[]{:S(2)}) collective-permute-start(f32[8,128]{1,0:T(8,128)S(1)} %get-tuple-element.49), channel_id=1, source_target_pairs={{16,32},{32,16},{48,64},{64,48},{80,96},{96,80},{112,0},{0,112},{1... | collective-permute-start | bytes 12296 | tf_op jit(solution)/shard_map/ppermute | solution.py:421
  14.8 24.5 %copy-start = (f32[1,128,2048]{2,1,0:T(8,128)S(1)}, f32[1,128,2048]{2,1,0:T(8,128)}, u32[]{:S(2)}) copy-start(f32[1,128,2048]{2,1,0:T(8,128)} %param.18) | copy-start | bytes 3145732
  39.5 2.5 %collective-permute-start.6 = (f32[1,128]{1,0:T(1,128)S(1)}, f32[1,128]{1,0:T(1,128)S(1)}, u32[]{:S(2)}, u32[]{:S(2)}) collective-permute-start(f32[1,128]{1,0:T(1,128)S(1)} %shard_map.117.refs_3_.d.disp), channel_id=1, source_target_pairs={{0,1},{1,0},{2,3},{3,2},{4,5},{5,4},{6,7},{7,6},{8,9},{9,8},{10,11... | collective-permute-start | bytes 1544 | tf_op jit(solution)/shard_map/ppermute | solution.py:422
  39.9 2.1 %collective-permute-start.7 = (f32[1,128]{1,0:T(1,128)S(1)}, f32[1,128]{1,0:T(1,128)S(1)}, u32[]{:S(2)}, u32[]{:S(2)}) collective-permute-start(f32[1,128]{1,0:T(1,128)S(1)} %shard_map.117.refs_3_.d.disp), channel_id=1, source_target_pairs={{1,2},{2,1},{3,4},{4,3},{5,6},{6,5},{7,8},{8,7},{9,10},{10,9},{11,... | collective-permute-start | bytes 1544 | tf_op jit(solution)/shard_map/ppermute | solution.py:421
  42.1 4.2 %collective-permute-start.8 = (f32[3,128]{1,0:T(4,128)S(1)}, f32[3,128]{1,0:T(4,128)S(1)}, u32[]{:S(2)}, u32[]{:S(2)}) collective-permute-start(f32[3,128]{1,0:T(4,128)S(1)} %shard_map.120), channel_id=1, source_target_pairs={{0,16},{16,0},{32,48},{48,32},{64,80},{80,64},{96,112},{112,96},{1... | collective-permute-start | bytes 4616 | tf_op jit(solution)/shard_map/ppermute | solution.py:422
  44.0 3.0 %collective-permute-start.9 = (f32[3,128]{1,0:T(4,128)S(1)}, f32[3,128]{1,0:T(4,128)S(1)}, u32[]{:S(2)}, u32[]{:S(2)}) collective-permute-start(f32[3,128]{1,0:T(4,128)S(1)} %shard_map.120), channel_id=1, source_target_pairs={{16,32},{32,16},{48,64},{64,48},{80,96},{96,80},{112,0},{0,112},{1... | collective-permute-start | bytes 4616 | tf_op jit(solution)/shard_map/ppermute | solution.py:421
